TPU v7x, 32 devices: a whole 2x2x4 slice. The times are simulated.
32 devices in a mesh: trial: 2 (over y), fsdp: 8 (over z, x), tensor: 2 (over core).
Axes of the slice: x: 2, y: 2, z: 4, core: 2. Of those that a mesh axis runs over, the one named last changes fastest.
Arguments:
- tokens: bfloat16 [4096, 4096], P(('trial', 'fsdp'), 'tensor'), parts along dimension 0, may hold values from -110 to 110
- norm_gain: float32 [4096], replicated, may hold values from 0.25 to 1.75
- grow_width: bfloat16 [4096, 2048], P('fsdp'), may hold values from -0.09375 to 0.09375
- old_value: bfloat16 [2048, 1024], P('fsdp', 'tensor'), may hold values from -0.125 to 0.125
- grow_head: bfloat16 [2048, 1024], P('tensor', 'fsdp'), may hold values from -0.1875 to 0.1875
- cotangent: bfloat16 [4096, 2048], P(('trial', 'fsdp'), 'tensor'), parts along dimension 0, may hold values from -6 to 6
Outputs:
- grown_value: bfloat16 [8192, 1024], P(('trial', 'fsdp'), 'tensor'), parts along dimension 0
- value_out: bfloat16 [4096, 2048], P(('trial', 'fsdp'), 'tensor'), parts along dimension 0
- head_grad: float32 [2048, 2048], P(('trial', 'fsdp'), 'tensor'), parts along dimension 0
There are 2 independent parts, one for each index of `trial`. A program takes and returns all parts, laid end to end along the dimension named above; an argument that names none is the same for every part. Nothing has to cross between parts.
All inputs are finite; a program needn't handle non-finite values.
Results may differ from a plain program's by a relative error of at most 0.0064.
Values may be sent and summed in bfloat16 or wider, within the bound.
A program may use at most 64 MiB of HBM per device.

v0:
```python
import math
import jax
import jax.numpy as jnp
from jax import lax
from jax.sharding import PartitionSpec as P


def per_device(tokens, norm_gain, grow_width, old_value, grow_head, cotangent):
    whole = lax.all_gather(tokens, "tensor", axis=1, tiled=True)
    widened = whole.astype(jnp.float32)
    meansq = jnp.mean(widened * widened, axis=-1, keepdims=True)
    normed = (widened * lax.rsqrt(meansq + 1e-05) * norm_gain).astype(jnp.bfloat16)
    old_rows = lax.all_gather(old_value, "tensor", axis=1, tiled=True)
    old_all = lax.all_gather(old_rows, "fsdp", axis=0, tiled=True)
    grown_slab = jnp.dot(grow_width, old_all, preferred_element_type=jnp.float32).astype(
        jnp.bfloat16
    )
    grown_full = lax.all_gather(grown_slab, "fsdp", axis=0, tiled=True)
    mixed = jnp.dot(normed, grown_full, preferred_element_type=jnp.float32).astype(jnp.bfloat16)
    half_width = old_all.shape[1] // lax.axis_size("tensor")
    grown_value = lax.dynamic_slice_in_dim(
        grown_slab, lax.axis_index("tensor") * half_width, half_width, 1
    )
    head_all = lax.all_gather(grow_head, "fsdp", axis=1, tiled=True)
    value_out = lax.dot_general(
        mixed, head_all, (((1,), (1,)), ((), ())), preferred_element_type=jnp.float32
    ).astype(jnp.bfloat16)
    summed = lax.psum_scatter(
        lax.dot_general(
            mixed, cotangent, (((0,), (0,)), ((), ())), preferred_element_type=jnp.float32
        ),
        "fsdp",
        scatter_dimension=0,
        tiled=True,
    )
    head_grad = summed * (1.0 / math.sqrt(tokens.shape[0] * lax.axis_size("fsdp")))
    return (grown_value, value_out, head_grad)


def solution(mesh):
    return jax.shard_map(
        per_device,
        mesh=mesh,
        in_specs=(
            P(("trial", "fsdp"), "tensor"),
            P(),
            P("fsdp", None),
            P("fsdp", "tensor"),
            P("tensor", "fsdp"),
            P(("trial", "fsdp"), "tensor"),
        ),
        out_specs=(
            P(("trial", "fsdp"), "tensor"),
            P(("trial", "fsdp"), "tensor"),
            P(("trial", "fsdp"), "tensor"),
        ),
        check_vma=False,
    )
```

profile of v0, /device:TPU:0, one launch (start us, length us, event | category | flops | bytes accessed | tf_op | source)
XLA Modules:
  0.0 375.4 jit_solution(16384810196821062314)
XLA Ops:
  7.2 0.0 copy-start
  7.2 0.0 all-gather.5.cloned.1.call-start
  7.2 4.3 %all_gather.15 = bf16[256,1024]{1,0:T(8,128)(2,1)} all-gather(bf16[256,512]{1,0:T(8,128)(2,1)} %param.9), channel_id=1, replica_groups=mesh['trial'=2,'fsdp'=8,'tensor'=2] {'tensor'}, dimensions={1}, use_global_device_ids=true | all-gather | bytes 786432 | tf_op jit(solution)/shard_map/all_gather | solution.py:13
  11.6 0.0 all-gather.5.cloned.1.call-update
  11.6 0.0 all-gather.7.cloned.1.call-start
  11.6 0.7 all-gather.7.cloned.1.call-update
  12.3 0.0 copy-start.4
  12.3 0.0 all-gather.9.cloned.1.call-start
  12.4 75.1 %all-gather.5.cloned.1.call-done = bf16[2048,1024]{1,0:T(8,128)(2,1)} async-done(((bf16[256,1024]{1,0:T(8,128)(2,1)}), bf16[2048,1024]{1,0:T(8,128)(2,1)}) %all-gather.5.cloned.1.call-update) | async-done | bytes 4194320 | tf_op jit(solution)/shard_map/all_gather | solution.py:14
  87.5 0.0 copy-done
  87.5 5.6 %convolution_convert_fusion = bf16[512,1024]{1,0:T(8,128)(2,1)} fusion(bf16[512,2048]{1,0:T(8,128)(2,1)S(1)} %copy-done, bf16[2048,1024]{1,0:T(8,128)(2,1)} %all-gather.5.cloned.1.call-done), kind=kOutput, calls=%fused_computation.8 | convolution fusion | flops 2148007936 | bytes 7340032 | tf_op jit(solution)/shard_map/dot_general | solution.py:15
  93.1 0.0 all-gather.9.cloned.1.call-update
  93.1 0.0 all-gather.11.cloned.1.call-start
  93.2 0.5 all-gather.11.cloned.1.call-update
  93.7 0.0 reduce-scatter.2.cloned.1.call-start
  93.7 4.2 %all-gather.7.cloned.1.call-done = bf16[256,4096]{1,0:T(8,128)(2,1)} async-done(((bf16[256,2048]{1,0:T(8,128)(2,1)}), bf16[256,4096]{1,0:T(8,128)(2,1)}) %all-gather.7.cloned.1.call-update) | async-done | bytes 2097168 | tf_op jit(solution)/shard_map/all_gather | solution.py:9
  97.9 2.1 fusion
  100.0 0.0 copy-start.3
  100.0 126.2 %all-gather.9.cloned.1.call-done = bf16[4096,1024]{1,0:T(8,128)(2,1)} async-done(((bf16[512,1024]{1,0:T(8,128)(2,1)}), bf16[4096,1024]{1,0:T(8,128)(2,1)}) %all-gather.9.cloned.1.call-update) | async-done | bytes 8388624 | tf_op jit(solution)/shard_map/all_gather | solution.py:18
  226.2 0.0 copy-done.4
  226.2 6.4 %fusion.7 = bf16[256,1024]{1,0:T(8,128)(2,1)S(1)} fusion(bf16[4096,1024]{1,0:T(8,128)(2,1)} %all-gather.9.cloned.1.call-done, bf16[256,4096]{1,0:T(8,128)(2,1)} %all-gather.7.cloned.1.call-done, f32[4096]{0:T(1024)S(1)} %copy-done.4, f32[256]{0:T(256)S(1)} %add_rsqrt_fusion), kind=kOutput, calls=%fused_computation.9 | convolution fusion | flops 2151940096 | bytes 11027456 | tf_op jit(solution)/shard_map/dot_general | solution.py:19
  232.6 0.0 copy-start.2
  232.6 0.8 copy-done.2
  233.4 0.0 copy-done.3
  233.4 2.7 fusion.10
  236.1 0.0 copy-start.1
  236.1 0.0 reduce-scatter.2.cloned.1.call-update
  236.1 1.2 copy-done.1
  237.3 0.8 constant_dynamic-slice_fusion
  238.2 39.2 %all-gather.11.cloned.1.call-done = bf16[1024,1024]{1,0:T(8,128)(2,1)} async-done(((bf16[1024,128]{1,0:T(8,128)(2,1)}), bf16[1024,1024]{1,0:T(8,128)(2,1)}) %all-gather.11.cloned.1.call-update) | async-done | bytes 2097168 | tf_op jit(solution)/shard_map/all_gather | solution.py:24
  277.4 3.3 convolution_convert_fusion.1
  280.7 86.3 %reduce-scatter.2.cloned.1.call-done = f32[128,1024]{1,0:T(8,128)} async-done(((f32[1024,1024]{1,0:T(8,128)}), f32[128,1024]{1,0:T(8,128)}) %reduce-scatter.2.cloned.1.call-update) | async-done | bytes 524304 | tf_op jit(solution)/shard_map/reduce_scatter | solution.py:28
  367.0 1.9 broadcast_multiply_fusion
  (1 shorter events, 0.0 us)
Async XLA Ops:
  7.2 80.4 %copy-start = (bf16[512,2048]{1,0:T(8,128)(2,1)S(1)}, bf16[512,2048]{1,0:T(8,128)(2,1)}, u32[]{:S(2)}) copy-start(bf16[512,2048]{1,0:T(8,128)(2,1)} %param.8) | copy-start | bytes 6291460
  7.2 80.3 %all-gather.5.cloned.1.call-start = ((), (), s32[]{:S(2)}) async-start(), calls=%async_computation.1 | async-start | bytes 4718592 | tf_op jit(solution)/shard_map/all_gather | solution.py:14
  11.6 86.4 %all-gather.7.cloned.1.call-start = ((), (), s32[]{:S(2)}) async-start(), calls=%async_computation.2 | async-start | bytes 3145728 | tf_op jit(solution)/shard_map/all_gather | solution.py:9
  12.3 213.9 %copy-start.4 = (f32[4096]{0:T(1024)S(1)}, f32[4096]{0:T(1024)}, u32[]{:S(2)}) copy-start(f32[4096]{0:T(1024)} %param.7) | copy-start | bytes 49156
  12.3 213.9 %all-gather.9.cloned.1.call-start = ((), (), s32[]{:S(2)}) async-start(), calls=%async_computation.3 | async-start | bytes 9437184 | tf_op jit(solution)/shard_map/all_gather | solution.py:18
  93.1 184.3 %all-gather.11.cloned.1.call-start = ((), (), s32[]{:S(2)}) async-start(), calls=%async_computation.4 | async-start | bytes 2359296 | tf_op jit(solution)/shard_map/all_gather | solution.py:24
  93.7 273.3 %reduce-scatter.2.cloned.1.call-start = ((), (), s32[]{:S(2)}) async-start(), calls=%async_computation.5 | async-start | bytes 4718592 | tf_op jit(solution)/shard_map/reduce_scatter | solution.py:28
  100.0 133.4 %copy-start.3 = (bf16[256,1024]{1,0:T(8,128)(2,1)S(1)}, bf16[256,1024]{1,0:T(8,128)(2,1)}, u32[]{:S(2)}) copy-start(bf16[256,1024]{1,0:T(8,128)(2,1)} %param.11) | copy-start | bytes 1572868
  232.6 0.8 copy-start.2
  236.1 1.2 copy-start.1
Sparse Core Ops, SparseCore 0:
  11.7 75.7 all-gather.4
  89.1 8.8 all-gather.6
  100.1 126.0 all-gather.8
  228.1 49.2 all-gather.10
  280.9 86.0 reduce-scatter.1
where the time goes:
time: 376 us; the launch traced here: 375 us
  waiting for transfers between devices  332 us (88%)
  matrix products  18 us (5%)
  between operations  13.8 us (4%)
  blocking collectives  4.33 us (1%)
  other arithmetic  3.98 us (1%)
    all_gather x1, waiting for transfers between devices, per_device(): grown_full = lax.all_gather(grown_slab, 'fsdp', axis=0, tiled=True)  126 us
    reduce_scatter x1, waiting for transfers between devices, per_device(): lax.psum_scatter(lax.dot_general(mixed, cotangent, (((0,), (0,)), ((), ()...  86.3 us
    all_gather x1, waiting for transfers between devices, per_device(): old_all = lax.all_gather(old_rows, 'fsdp', axis=0, tiled=True)  75.1 us
    all_gather x1, waiting for transfers between devices, per_device(): head_all = lax.all_gather(grow_head, 'fsdp', axis=1, tiled=True)  39.2 us
  transfers between devices with their start and end apart: 5, of which 5 were waited for; matrix products, arithmetic and copies ran while one was open for 6% of the time, Pallas kernels for 0%

commit v1 on v0

--- a/solution.py
+++ b/solution.py
@@ -3,6 +3,17 @@
 import jax.numpy as jnp
 from jax import lax
 from jax.sharding import PartitionSpec as P
+
+
+def gather_by_hops(x, axis, along):
+    count = lax.axis_size(axis)
+    right = [(i, (i + 1) % count) for i in range(count)]
+    blocks = [x]
+    for hop in range(1, count):
+        blocks = [lax.ppermute(blocks[0], axis, right), *blocks]
+    full = jnp.concatenate(blocks, axis=along)
+    shift = (lax.axis_index(axis) + 1) * blocks[-1].shape[along]
+    return jnp.roll(full, shift, axis=along)
 
 
 def per_device(tokens, norm_gain, grow_width, old_value, grow_head, cotangent):
@@ -15,7 +26,7 @@
     grown_slab = jnp.dot(grow_width, old_all, preferred_element_type=jnp.float32).astype(
         jnp.bfloat16
     )
-    grown_full = lax.all_gather(grown_slab, "fsdp", axis=0, tiled=True)
+    grown_full = gather_by_hops(grown_slab, "fsdp", 0)
     mixed = jnp.dot(normed, grown_full, preferred_element_type=jnp.float32).astype(jnp.bfloat16)
     half_width = old_all.shape[1] // lax.axis_size("tensor")
     grown_value = lax.dynamic_slice_in_dim(

time: 376 us -> 398 us (1.059)
  local copies, waits for them, and re-layouts: 2.83 us -> 19.3 us
  waiting for transfers between devices: 332 us -> 340 us
  matrix products: 18 us -> 12.9 us
    ppermute x0 -> x7, waiting for transfers between devices: none -> 172 us  [gather_by_hops(): blocks = [lax.ppermute(blocks[0], axis, right), *blocks]]
    all_gather x1 -> x0, waiting for transfers between devices: 126 us -> none  [per_device(): grown_full = lax.all_gather(grown_slab, 'fsdp', axis=0, tiled=True)]
    all_gather x1, waiting for transfers between devices: 39.2 us -> 5.73 us  [per_device(): head_all = lax.all_gather(grow_head, 'fsdp', axis=1, tiled=True)]
    unnamed x10 -> x37, local copies, waits for them, and re-layouts: 2 us -> 18.4 us
    all_gather x1, waiting for transfers between devices: 4.2 us -> 0.03 us  [per_device(): whole = lax.all_gather(tokens, 'tensor', axis=1, tiled=True)]
  transfers between devices with their start and end apart: 5 -> 11, of which waited for: 5 -> 10; matrix products, arithmetic and copies ran while one was open for 6% -> 7% of each run, Pallas kernels for 0% -> 0%
where the time goes in v1:
time: 398 us; the launch traced here: 397 us
  waiting for transfers between devices  340 us (85%)
  local copies, waits for them, and re-layouts  19.3 us (5%)
  between operations  15.9 us (4%)
  matrix products  12.9 us (3%)
  blocking collectives  4.3 us (1%)
  other arithmetic  4.13 us (1%)
    ppermute x7, waiting for transfers between devices, gather_by_hops(): blocks = [lax.ppermute(blocks[0], axis, right), *blocks]  172 us
    reduce_scatter x1, waiting for transfers between devices, per_device(): lax.psum_scatter(lax.dot_general(mixed, cotangent, (((0,), (0,)), ((), ()...  86.2 us
    all_gather x1, waiting for transfers between devices, per_device(): old_all = lax.all_gather(old_rows, 'fsdp', axis=0, tiled=True)  75.9 us
    unnamed x37, local copies, waits for them, and re-layouts  18.4 us
  transfers between devices with their start and end apart: 11, of which 10 were waited for; matrix products, arithmetic and copies ran while one was open for 7% of the time, Pallas kernels for 0%

profile of v1, /device:TPU:0, one launch (start us, length us, event | category | flops | bytes accessed | tf_op | source)
XLA Modules:
  0.0 397.3 jit_solution(7949012790039925807)
XLA Ops:
  8.0 0.0 copy-start
  8.0 0.0 all-gather.4.cloned.1.call-start
  8.1 4.3 %all_gather.12 = bf16[256,1024]{1,0:T(8,128)(2,1)} all-gather(bf16[256,512]{1,0:T(8,128)(2,1)} %param.9), channel_id=1, replica_groups=mesh['trial'=2,'fsdp'=8,'tensor'=2] {'tensor'}, dimensions={1}, use_global_device_ids=true | all-gather | bytes 786432 | tf_op jit(solution)/shard_map/all_gather | solution.py:24
  12.4 0.0 all-gather.4.cloned.1.call-update
  12.4 0.0 all-gather.6.cloned.1.call-start
  12.4 75.9 %all-gather.4.cloned.1.call-done = bf16[2048,1024]{1,0:T(8,128)(2,1)} async-done(((bf16[256,1024]{1,0:T(8,128)(2,1)}), bf16[2048,1024]{1,0:T(8,128)(2,1)}) %all-gather.4.cloned.1.call-update) | async-done | bytes 4194320 | tf_op jit(solution)/shard_map/all_gather | solution.py:25
  88.4 0.0 copy-done
  88.4 4.5 %convolution_convert_fusion = bf16[512,1024]{1,0:T(8,128)(2,1)S(1)} fusion(bf16[512,2048]{1,0:T(8,128)(2,1)S(1)} %copy-done, bf16[2048,1024]{1,0:T(8,128)(2,1)} %all-gather.4.cloned.1.call-done), kind=kOutput, calls=%fused_computation.9 | convolution fusion | flops 2148007936 | bytes 7340032 | tf_op jit(solution)/shard_map/dot_general | solution.py:26
  92.9 0.6 collective-permute-start
  93.5 25.9 %collective-permute-done = bf16[512,1024]{1,0:T(8,128)(2,1)S(1)} collective-permute-done((bf16[512,1024]{1,0:T(8,128)(2,1)S(1)}, bf16[512,1024]{1,0:T(8,128)(2,1)S(1)}, u32[]{:S(2)}, u32[]{:S(2)}) %collective-permute-start) | collective-permute-done | bytes 1048608 | tf_op jit(solution)/shard_map/ppermute | solution.py:13
  119.4 1.0 copy-done.1
  120.3 0.0 collective-permute-start.1
  120.3 25.5 %collective-permute-done.1 = bf16[512,1024]{1,0:T(8,128)(2,1)S(1)} collective-permute-done((bf16[512,1024]{1,0:T(8,128)(2,1)S(1)}, bf16[512,1024]{1,0:T(8,128)(2,1)S(1)}, u32[]{:S(2)}, u32[]{:S(2)}) %collective-permute-start.1) | collective-permute-done | bytes 1048608 | tf_op jit(solution)/shard_map/ppermute | solution.py:13
  145.8 1.0 copy-done.3
  146.8 0.0 collective-permute-start.2
  146.8 24.6 %collective-permute-done.2 = bf16[512,1024]{1,0:T(8,128)(2,1)S(1)} collective-permute-done((bf16[512,1024]{1,0:T(8,128)(2,1)S(1)}, bf16[512,1024]{1,0:T(8,128)(2,1)S(1)}, u32[]{:S(2)}, u32[]{:S(2)}) %collective-permute-start.2) | collective-permute-done | bytes 1048608 | tf_op jit(solution)/shard_map/ppermute | solution.py:13
  171.4 1.0 copy-done.5
  172.3 0.0 collective-permute-start.3
  172.4 23.7 %collective-permute-done.3 = bf16[512,1024]{1,0:T(8,128)(2,1)} collective-permute-done((bf16[512,1024]{1,0:T(8,128)(2,1)S(1)}, bf16[512,1024]{1,0:T(8,128)(2,1)}, u32[]{:S(2)}, u32[]{:S(2)}) %collective-permute-start.3) | collective-permute-done | bytes 1048608 | tf_op jit(solution)/shard_map/ppermute | solution.py:13
  196.1 0.0 collective-permute-start.4
  196.1 0.0 all-gather.6.cloned.1.call-update
  196.1 0.0 all-gather.8.cloned.1.call-start
  196.2 23.2 %collective-permute-done.4 = bf16[512,1024]{1,0:T(8,128)(2,1)} collective-permute-done((bf16[512,1024]{1,0:T(8,128)(2,1)}, bf16[512,1024]{1,0:T(8,128)(2,1)}, u32[]{:S(2)}, u32[]{:S(2)}) %collective-permute-start.4) | collective-permute-done | bytes 1048608 | tf_op jit(solution)/shard_map/ppermute | solution.py:13
  219.4 0.0 collective-permute-start.5
  219.4 23.3 %collective-permute-done.5 = bf16[512,1024]{1,0:T(8,128)(2,1)} collective-permute-done((bf16[512,1024]{1,0:T(8,128)(2,1)}, bf16[512,1024]{1,0:T(8,128)(2,1)}, u32[]{:S(2)}, u32[]{:S(2)}) %collective-permute-start.5) | collective-permute-done | bytes 1048608 | tf_op jit(solution)/shard_map/ppermute | solution.py:13
  242.7 0.0 collective-permute-start.6
  242.8 0.0 all-gather.8.cloned.1.call-update
  242.8 0.0 reduce-scatter.2.cloned.1.call-start
  242.8 0.0 all-gather.6.cloned.1.call-done
  242.9 0.0 copy-start.6
  242.9 0.0 copy-start.4
  242.9 0.0 copy-start.2
  242.9 2.2 fusion.2
  245.2 0.0 copy-start.10
  245.2 25.7 %collective-permute-done.6 = bf16[512,1024]{1,0:T(8,128)(2,1)} collective-permute-done((bf16[512,1024]{1,0:T(8,128)(2,1)}, bf16[512,1024]{1,0:T(8,128)(2,1)}, u32[]{:S(2)}, u32[]{:S(2)}) %collective-permute-start.6) | collective-permute-done | bytes 1048608 | tf_op jit(solution)/shard_map/ppermute | solution.py:13
  270.9 1.3 constant_dynamic-update-slice_fusion.15
  272.2 1.3 constant_dynamic-update-slice_fusion.14
  273.5 1.3 constant_dynamic-update-slice_fusion.13
  274.8 1.3 constant_dynamic-update-slice_fusion.12
  276.1 1.3 constant_dynamic-update-slice_fusion.11
  277.4 1.3 constant_dynamic-update-slice_fusion.10
  278.7 1.3 constant_dynamic-update-slice_fusion.9
  280.0 0.0 copy-start.9
  280.1 0.1 constant_dynamic-update-slice_fusion.8
  280.1 1.3 constant_dynamic-update-slice_fusion.7
  281.5 1.3 constant_dynamic-update-slice_fusion.6
  282.8 1.3 constant_dynamic-update-slice_fusion.5
  284.1 1.3 constant_dynamic-update-slice_fusion.4
  285.4 0.0 copy-done.6
  285.4 0.1 constant_dynamic-update-slice_fusion.3
  285.5 0.0 copy-done.4
  285.5 0.1 constant_dynamic-update-slice_fusion.2
  285.6 0.1 constant_dynamic-update-slice_fusion.1
  285.6 0.1 constant_dynamic-update-slice_fusion
  285.7 2.4 fusion.8
  288.2 0.0 copy-start.8
  288.2 0.8 copy-done.8
  289.0 2.7 fusion.14
  291.7 0.0 reduce-scatter.2.cloned.1.call-update
  291.7 0.8 constant_dynamic-slice_fusion
  292.5 5.7 %all-gather.8.cloned.1.call-done = bf16[1024,1024]{1,0:T(8,128)(2,1)} async-done(((bf16[1024,128]{1,0:T(8,128)(2,1)}), bf16[1024,1024]{1,0:T(8,128)(2,1)}) %all-gather.8.cloned.1.call-update) | async-done | bytes 2097168 | tf_op jit(solution)/shard_map/all_gather | solution.py:35
  298.3 3.3 convolution_convert_fusion.1
  301.6 86.2 %reduce-scatter.2.cloned.1.call-done = f32[128,1024]{1,0:T(8,128)} async-done(((f32[1024,1024]{1,0:T(8,128)}), f32[128,1024]{1,0:T(8,128)}) %reduce-scatter.2.cloned.1.call-update) | async-done | bytes 524304 | tf_op jit(solution)/shard_map/reduce_scatter | solution.py:39
  387.8 1.9 broadcast_multiply_fusion
  (9 shorter events, 0.0 us)
Async XLA Ops:
  8.0 80.4 %copy-start = (bf16[512,2048]{1,0:T(8,128)(2,1)S(1)}, bf16[512,2048]{1,0:T(8,128)(2,1)}, u32[]{:S(2)}) copy-start(bf16[512,2048]{1,0:T(8,128)(2,1)} %param.8) | copy-start | bytes 6291460
  8.0 80.3 %all-gather.4.cloned.1.call-start = ((), (), s32[]{:S(2)}) async-start(), calls=%async_computation.1 | async-start | bytes 4718592 | tf_op jit(solution)/shard_map/all_gather | solution.py:25
  12.4 230.5 %all-gather.6.cloned.1.call-start = ((), (), s32[]{:S(2)}) async-start(), calls=%async_computation.2 | async-start | bytes 3145728 | tf_op jit(solution)/shard_map/all_gather | solution.py:20
  92.9 26.5 %collective-permute-start = (bf16[512,1024]{1,0:T(8,128)(2,1)S(1)}, bf16[512,1024]{1,0:T(8,128)(2,1)S(1)}, u32[]{:S(2)}, u32[]{:S(2)}) collective-permute-start(bf16[512,1024]{1,0:T(8,128)(2,1)S(1)} %convolution_convert_fusion), channel_id=1, source_target_pairs={{0,2},{2,4},{4,6},{6,8},{8,10},{10,12},{12,14},{14,0},{1,3},{3,5},... | collective-permute-start | bytes 3145736 | tf_op jit(solution)/shard_map/ppermute | solution.py:13
  119.3 1.0 copy-start.1
  120.3 25.5 %collective-permute-start.1 = (bf16[512,1024]{1,0:T(8,128)(2,1)S(1)}, bf16[512,1024]{1,0:T(8,128)(2,1)S(1)}, u32[]{:S(2)}, u32[]{:S(2)}) collective-permute-start(bf16[512,1024]{1,0:T(8,128)(2,1)S(1)} %collective-permute-done), channel_id=1, source_target_pairs={{0,2},{2,4},{4,6},{6,8},{8,10},{10,12},{12,14},{14,0},{1,3},{3,5},... | collective-permute-start | bytes 3145736 | tf_op jit(solution)/shard_map/ppermute | solution.py:13
  145.8 1.0 copy-start.3
  146.8 24.6 %collective-permute-start.2 = (bf16[512,1024]{1,0:T(8,128)(2,1)S(1)}, bf16[512,1024]{1,0:T(8,128)(2,1)S(1)}, u32[]{:S(2)}, u32[]{:S(2)}) collective-permute-start(bf16[512,1024]{1,0:T(8,128)(2,1)S(1)} %collective-permute-done.1), channel_id=1, source_target_pairs={{0,2},{2,4},{4,6},{6,8},{8,10},{10,12},{12,14},{14,0},{1,3},{3,5},... | collective-permute-start | bytes 3145736 | tf_op jit(solution)/shard_map/ppermute | solution.py:13
  171.4 1.0 copy-start.5
  172.3 23.8 %collective-permute-start.3 = (bf16[512,1024]{1,0:T(8,128)(2,1)S(1)}, bf16[512,1024]{1,0:T(8,128)(2,1)}, u32[]{:S(2)}, u32[]{:S(2)}) collective-permute-start(bf16[512,1024]{1,0:T(8,128)(2,1)S(1)} %collective-permute-done.2), channel_id=1, source_target_pairs={{0,2},{2,4},{4,6},{6,8},{8,10},{10,12},{12,14},{14,0},{1,3},{3,5},... | collective-permute-start | bytes 3145736 | tf_op jit(solution)/shard_map/ppermute | solution.py:13
  196.1 23.3 %collective-permute-start.4 = (bf16[512,1024]{1,0:T(8,128)(2,1)}, bf16[512,1024]{1,0:T(8,128)(2,1)}, u32[]{:S(2)}, u32[]{:S(2)}) collective-permute-start(bf16[512,1024]{1,0:T(8,128)(2,1)} %collective-permute-done.3), channel_id=1, source_target_pairs={{0,2},{2,4},{4,6},{6,8},{8,10},{10,12},{12,14},{14,0},{1,3},{3,5},... | collective-permute-start | bytes 3145736 | tf_op jit(solution)/shard_map/ppermute | solution.py:13
  196.1 102.1 %all-gather.8.cloned.1.call-start = ((), (), s32[]{:S(2)}) async-start(), calls=%async_computation.3 | async-start | bytes 2359296 | tf_op jit(solution)/shard_map/all_gather | solution.py:35
  219.4 23.3 %collective-permute-start.5 = (bf16[512,1024]{1,0:T(8,128)(2,1)}, bf16[512,1024]{1,0:T(8,128)(2,1)}, u32[]{:S(2)}, u32[]{:S(2)}) collective-permute-start(bf16[512,1024]{1,0:T(8,128)(2,1)} %collective-permute-done.4), channel_id=1, source_target_pairs={{0,2},{2,4},{4,6},{6,8},{8,10},{10,12},{12,14},{14,0},{1,3},{3,5},... | collective-permute-start | bytes 3145736 | tf_op jit(solution)/shard_map/ppermute | solution.py:13
  242.7 28.1 %collective-permute-start.6 = (bf16[512,1024]{1,0:T(8,128)(2,1)}, bf16[512,1024]{1,0:T(8,128)(2,1)}, u32[]{:S(2)}, u32[]{:S(2)}) collective-permute-start(bf16[512,1024]{1,0:T(8,128)(2,1)} %collective-permute-done.5), channel_id=1, source_target_pairs={{0,2},{2,4},{4,6},{6,8},{8,10},{10,12},{12,14},{14,0},{1,3},{3,5},... | collective-permute-start | bytes 3145736 | tf_op jit(solution)/shard_map/ppermute | solution.py:13
  242.8 145.0 %reduce-scatter.2.cloned.1.call-start = ((), (), s32[]{:S(2)}) async-start(), calls=%async_computation.4 | async-start | bytes 4718592 | tf_op jit(solution)/shard_map/reduce_scatter | solution.py:39
  242.9 42.5 %copy-start.6 = (bf16[512,1024]{1,0:T(8,128)(2,1)S(1)}, bf16[512,1024]{1,0:T(8,128)(2,1)}, u32[]{:S(2)}) copy-start(bf16[512,1024]{1,0:T(8,128)(2,1)} %copy-done.5) | copy-start | bytes 3145732
  242.9 42.6 %copy-start.4 = (bf16[512,1024]{1,0:T(8,128)(2,1)S(1)}, bf16[512,1024]{1,0:T(8,128)(2,1)}, u32[]{:S(2)}) copy-start(bf16[512,1024]{1,0:T(8,128)(2,1)} %copy-done.3) | copy-start | bytes 3145732
  242.9 42.7 %copy-start.2 = (bf16[512,1024]{1,0:T(8,128)(2,1)S(1)}, bf16[512,1024]{1,0:T(8,128)(2,1)}, u32[]{:S(2)}) copy-start(bf16[512,1024]{1,0:T(8,128)(2,1)} %copy-done.1) | copy-start | bytes 3145732
  245.2 40.6 %copy-start.7 = (bf16[256,4096]{1,0:T(8,128)(2,1)S(1)}, bf16[256,4096]{1,0:T(8,128)(2,1)}, u32[]{:S(2)}) copy-start(bf16[256,4096]{1,0:T(8,128)(2,1)} %all-gather.6.cloned.1.call-done) | copy-start | bytes 6291460
  245.2 40.6 %copy-start.10 = (f32[4096]{0:T(1024)S(1)}, f32[4096]{0:T(1024)}, u32[]{:S(2)}) copy-start(f32[4096]{0:T(1024)} %param.7) | copy-start | bytes 49156
  280.0 8.9 %copy-start.9 = (bf16[256,1024]{1,0:T(8,128)(2,1)S(1)}, bf16[256,1024]{1,0:T(8,128)(2,1)}, u32[]{:S(2)}) copy-start(bf16[256,1024]{1,0:T(8,128)(2,1)} %param.11) | copy-start | bytes 1572868
  288.2 0.8 copy-start.8
Sparse Core Ops, SparseCore 0:
  12.5 75.8 all-gather.3
Sparse Core Ops, SparseCore 1:
  196.2 11.8 all-gather.5
  242.9 55.4 all-gather.7
  301.8 86.0 reduce-scatter.1
